TPU v7x, 128 devices: a whole 4x4x4 slice. The times are simulated.
128 devices in a mesh: row: 16 (over z, x), col: 8 (over y, core).
Axes of the slice: x: 4, y: 4, z: 4, core: 2. Of those that a mesh axis runs over, the one named last changes fastest.
Arguments:
- amplitudes: float32 [12288, 6144], P('row', 'col'), may hold values from -6 to 6
- integrals: float32 [6144, 6144], P('col', 'row'), may hold values from -0.125 to 0.125
- flags: int32 [64, 64], replicated, may hold values from 0 to 1, as said below
Outputs:
- ladder: float32 [12288, 6144], P('row', 'col')
Inputs may be any that keep to these rules, and one draw needn't show every extreme that they name: `flags`: in each aligned block of 8 a-tiles by 4 d-tiles (tile rows k * 8 onward, tile columns m * 4 onward) at least 6 and at most 19 tile pairs are listed, and some block lists exactly 19.
All inputs are finite; a program needn't handle non-finite values.
Results may differ from a plain program's by a relative error of at most 0.00007.
Values sent between devices are 32-bit elements; how exact they have to be, the bound alone decides.
A program may use at most 192 MiB of HBM per device.

v0:
```python
import jax
import jax.numpy as jnp
from jax import lax
from jax.sharding import PartitionSpec as P

TILE = 96


def body(amplitudes, integrals, flags):
    row_index = lax.axis_index("row")
    col_index = lax.axis_index("col")
    a_extent, d_extent = integrals.shape
    a_tiles = a_extent // TILE
    d_tiles = d_extent // TILE
    own_flags = lax.dynamic_slice(
        flags, (col_index * a_tiles, row_index * d_tiles), (a_tiles, d_tiles)
    )
    weights = own_flags.astype(jnp.float32)[:, None, :, None]
    screened = (integrals.reshape(a_tiles, TILE, d_tiles, TILE) * weights).reshape(
        a_extent, d_extent
    )
    panel = lax.all_gather(screened, "row", axis=1, tiled=True)
    return lax.dot_general(
        lax.all_gather(amplitudes, "col", axis=1, tiled=True),
        panel,
        (((1,), (1,)), ((), ())),
        precision=lax.Precision.HIGHEST,
        preferred_element_type=jnp.float32,
    )


def solution(mesh):
    return jax.shard_map(
        body,
        mesh=mesh,
        in_specs=(P("row", "col"), P("col", "row"), P()),
        out_specs=P("row", "col"),
        check_vma=False,
    )
```

profile of v0, /device:TPU:1, one launch (start us, length us, event | category | flops | bytes accessed | tf_op | source)
XLA Modules:
  0.0 289.8 jit_solution(13019698028074702139)
XLA Ops:
  6.5 0.0 all-gather.5.cloned.1.call-start
  6.5 0.7 all-gather.5.cloned.1.call-update
  7.3 0.0 all-gather.3.cloned.1.call-start
  7.3 0.8 dynamic-slice_convert_fusion
  8.1 0.3 mul.19
  8.4 0.8 mul.20
  9.1 2.4 mul.21
  11.5 0.0 all-gather.3.cloned.1.call-update
  11.6 94.9 %all-gather.5.cloned.1.call-done = f32[768,6144]{1,0:T(8,128)} async-done(((f32[768,768]{1,0:T(8,128)}), f32[768,6144]{1,0:T(8,128)}) %all-gather.5.cloned.1.call-update) | async-done | bytes 18874384 | tf_op jit(solution)/shard_map/all_gather | solution.py:24
  106.5 124.7 %all-gather.3.cloned.1.call-done = f32[768,6144]{1,0:T(8,128)} async-done(((f32[768,384]{1,0:T(8,128)}), f32[768,6144]{1,0:T(8,128)}) %all-gather.3.cloned.1.call-update) | async-done | bytes 18874384 | tf_op jit(solution)/shard_map/all_gather | solution.py:22
  231.2 49.8 %convolution_bitcast_fusion = f32[768,768]{0,1:T(8,128)S(1)} fusion(f32[768,6144]{1,0:T(8,128)} %all-gather.3.cloned.1.call-done, f32[768,6144]{1,0:T(8,128)} %all-gather.5.cloned.1.call-done), kind=kOutput, calls=%fused_computation | convolution fusion | flops 43486543872 | bytes 40108032 | tf_op jit(solution)/shard_map/dot_general | solution.py:23
  281.0 2.0 copy.4
Async XLA Ops:
  6.5 99.9 %all-gather.5.cloned.1.call-start = ((), (), s32[]{:S(2)}) async-start(), calls=%async_computation.1 | async-start | bytes 21233664 | tf_op jit(solution)/shard_map/all_gather | solution.py:24
  7.3 223.9 %all-gather.3.cloned.1.call-start = ((), (), s32[]{:S(2)}) async-start(), calls=%async_computation | async-start | bytes 20054016 | tf_op jit(solution)/shard_map/all_gather | solution.py:22
Sparse Core Ops, SparseCore 0:
  9.0 97.3 all-gather.4
  108.7 122.4 all-gather.2
where the time goes:
time: 290 us
  waiting for transfers between devices  220 us (76%)
  matrix products  49.8 us (17%)
  between operations  13.4 us (5%)
  other arithmetic  3.17 us (1%)
  local copies, waits for them, and re-layouts  3 us (1%)
    all_gather x1, waiting for transfers between devices, body(): panel = lax.all_gather(screened, 'row', axis=1, tiled=True)  125 us
    all_gather x1, waiting for transfers between devices, body(): lax.all_gather(amplitudes, 'col', axis=1, tiled=True)  94.9 us
    dot_general x1, matrix products, body(): lax.dot_general(lax.all_gather(amplitudes, 'col', axis=1, tiled=True), pa...  49.8 us
  transfers between devices with their start and end apart: 2, of which 2 were waited for; matrix products, arithmetic and copies ran while one was open for 1% of the time, Pallas kernels for 0%

commit v1 on v0

v1 whole, which is shorter than its diff:
```python
import jax
import jax.numpy as jnp
from jax import lax
from jax.experimental import pallas as pl
from jax.experimental.pallas import tpu as pltpu
from jax.sharding import PartitionSpec as P

TILE = 96
CAP = 19
PIECE = 24
PIECES = 3 * CAP
MESH = pl.DeviceIdType.MESH
CHUNKS = 8
CHUNK = 96

FIRST, SECOND = (0, 29), (29, 28)
PASS_UP = {FIRST: (0, 14), SECOND: (29, 14)}
PASS_DOWN = {FIRST: (14, 15), SECOND: (43, 14)}


def lanes_of(rows):
    return lax.broadcasted_iota(jnp.int32, (rows, 128), 1)


def pack_kernel(flags_smem, flags_ref, x_ref, packed_ref, table_ref, turned):
    row, col = lax.axis_index("row"), lax.axis_index("col")
    own = flags_ref[pl.ds(pl.multiple_of(col * 8, 8), 8), :].astype(jnp.float32)
    d_from = lax.broadcasted_iota(jnp.int32, (64, 64), 0)
    d_to = lax.broadcasted_iota(jnp.int32, (64, 64), 1)
    earlier = ((d_from // 4 == d_to // 4) & (d_from < d_to)).astype(jnp.float32)
    i_to = lax.broadcasted_iota(jnp.int32, (8, 8), 0)
    i_from = lax.broadcasted_iota(jnp.int32, (8, 8), 1)
    above = (i_from < i_to).astype(jnp.float32)
    before = jnp.dot(own, earlier, preferred_element_type=jnp.float32)
    rank = jnp.dot(above, own, preferred_element_type=jnp.float32) + jnp.sum(before, axis=0, keepdims=True)
    table_ref[...] = (jnp.where(own > 0.5, rank, float(CAP)) * 3.0).astype(jnp.int32)

    packed_ref[...] = jnp.zeros_like(packed_ref)
    turned[...] = x_ref[...].T
    lane = lanes_of(TILE)
    count = jnp.int32(0)
    for j in range(4):
        for i in range(8):
            flag = flags_smem[col * 8 + i, row * 4 + j]

            @pl.when(flag != 0)
            def _():
                rows = slice(j * TILE, (j + 1) * TILE)
                first, offset = divmod(i * TILE, 128)
                tile = turned[rows, first * 128 : first * 128 + 128]
                if offset:
                    tile = pltpu.roll(tile, 128 - offset, 1)
                if offset > 32:
                    right = pltpu.roll(turned[rows, first * 128 + 128 : first * 128 + 256], 128 - offset, 1)
                    tile = jnp.where(lane < 128 - offset, tile, right)
                last = tile[3 * PIECE :]
                for q in range(3):
                    piece = tile[q * PIECE : (q + 1) * PIECE]
                    packed_ref[3 * count + q] = jnp.where(
                        lanes_of(PIECE) < TILE, piece, pltpu.roll(last, 96 - 32 * q, 1))

            count = count + flag


def split(value):
    high = value.astype(jnp.bfloat16)
    low = (value - high.astype(jnp.float32)).astype(jnp.bfloat16)
    return high, low


def main_kernel(table, amp_hbm, packed_hbm, out_ref, amp, b_high, b_low, *rest):
    blocks = {(dx, dz): rest[dx * 4 + dz] for dx in range(4) for dz in range(4)}
    send_sem, recv_sem, local_sem = rest[16:]
    row, col = lax.axis_index("row"), lax.axis_index("col")
    x, z = lax.rem(row, 4), lax.div(row, 4)
    k, y = lax.rem(col, 2), lax.div(col, 2)

    def at_x(d):
        return (z * 4 + lax.rem(x + d, 4), col)

    def at_z(d):
        return (lax.rem(z + d, 4) * 4 + x, col)

    def at_y(d):
        return (row, lax.rem(y + d, 4) * 2 + k)

    mate = (row, y * 2 + 1 - k)

    def column_of(d, core):
        return lax.rem(y + d, 4) * 2 + core

    barrier = pltpu.get_barrier_semaphore()
    for peer in (at_x(1), at_x(3), at_z(1), at_z(3), at_y(1), at_y(3), mate):
        pl.semaphore_signal(barrier, inc=1, device_id=peer, device_id_type=MESH)
    pl.semaphore_wait(barrier, 7)

    started = []

    def send(src, dst, device):
        n = len(started)
        copy = pltpu.make_async_remote_copy(
            src_ref=src, dst_ref=dst, send_sem=send_sem.at[n], recv_sem=recv_sem.at[n],
            device_id=device, device_id_type=MESH,
        )
        copy.start()
        started.append(copy)
        return copy

    def rows_of(q):
        return pl.ds(q * CHUNK, CHUNK)

    up, down, pass_up, pass_down, shared = {}, {}, {}, {}, {}
    up_order, down_order = (0, 1, 2, 3, 4, 5, 6, 7), (4, 5, 6, 7, 0, 1, 2, 3)

    def send_own(n):
        q = up_order[n]
        up[q] = send(amp_hbm.at[rows_of(q)], amp.at[col, rows_of(q)], at_y(1))
        q = down_order[n]
        down[q] = send(amp_hbm.at[rows_of(q)], amp.at[col, rows_of(q)], at_y(3))

    def part(ref, span):
        return ref.at[pl.ds(span[0], span[1])]

    ring = {}

    def key_of(half, phase, other, d):
        along_x = (half is FIRST) == (phase == 1)
        return (d, other) if along_x else (other, d)

    def peer_of(half, phase, d):
        return at_x(d) if (half is FIRST) == (phase == 1) else at_z(d)

    def ring_send(half, phase, other):
        own = key_of(half, phase, other, 0)
        src = packed_hbm if own == (0, 0) else blocks[own]
        ring[half, phase, other, "up"] = send(
            part(src, half), part(blocks[key_of(half, phase, other, 3)], half), peer_of(half, phase, 1))
        ring[half, phase, other, "down"] = send(
            part(src, half), part(blocks[key_of(half, phase, other, 1)], half), peer_of(half, phase, 3))

    def ring_pass(half, phase, other):
        ring[half, phase, other, "up"].wait_recv()
        far = blocks[key_of(half, phase, other, 2)]
        span = PASS_UP[half]
        ring[half, phase, other, "pass_up"] = send(
            part(blocks[key_of(half, phase, other, 3)], span), part(far, span), peer_of(half, phase, 1))
        ring[half, phase, other, "down"].wait_recv()
        span = PASS_DOWN[half]
        ring[half, phase, other, "pass_down"] = send(
            part(blocks[key_of(half, phase, other, 1)], span), part(far, span), peer_of(half, phase, 3))

    def ring_last(half, phase, other):
        ring[half, phase, other, "pass_up"].wait_recv()
        ring[half, phase, other, "pass_down"].wait_recv()

    halves = (FIRST, SECOND)

    send_own(0)
    for half in halves:
        ring_send(half, 1, 0)
    for half in halves:
        ring_send(half, 2, 0)
    own_amp = pltpu.make_async_copy(amp_hbm, amp.at[col], local_sem.at[0])
    own_amp.start()
    own_block = pltpu.make_async_copy(packed_hbm, blocks[0, 0].at[pl.ds(0, PIECES)], local_sem.at[1])
    own_block.start()
    for n in range(1, CHUNKS):
        send_own(n)
    shared["own"] = send(amp_hbm, amp.at[col], mate)

    def share(key, column, q):
        shared[key] = send(amp.at[column, rows_of(q)], amp.at[column, rows_of(q)], mate)

    def y_step(n):
        below, above = column_of(3, k), column_of(1, k)
        q = up_order[n]
        up[q].wait_recv()
        if n < 4:
            pass_up[q] = send(amp.at[below, rows_of(q)], amp.at[below, rows_of(q)], at_y(1))
        share(("below", q), below, q)
        q = down_order[n]
        down[q].wait_recv()
        if n < 4:
            pass_down[q] = send(amp.at[above, rows_of(q)], amp.at[above, rows_of(q)], at_y(3))
        share(("above", q), above, q)

    def y_last(n):
        far = column_of(2, k)
        q = up_order[n]
        pass_up[q].wait_recv()
        share(("far", q), far, q)
        q = down_order[n]
        pass_down[q].wait_recv()
        share(("far", q), far, q)

    lane24, lane96 = lanes_of(PIECE), lanes_of(TILE)

    def unpack(dx, dz):
        block = blocks[dx, dz]
        xs, zs = lax.rem(x + dx, 4), lax.rem(z + dz, 4)
        source = zs * 4 + xs
        column = lax.div(source, 2)
        base = lax.rem(source, 2) * 384

        @pl.loop(0, 4)
        def _(j):
            target = pl.ds(pl.multiple_of(base + j * TILE, 32), TILE)
            for group in range(2):
                tiles = []
                for i in range(4):
                    start = table[group * 4 + i, source * 4 + j]
                    pieces = [block[start + q] for q in range(3)]
                    turned = [pltpu.roll(pieces[q], 32 + 32 * q, 1) for q in range(3)]
                    last = jnp.where(lane24 < 32, turned[0], jnp.where(lane24 < 64, turned[1], turned[2]))
                    tile = jnp.concatenate(pieces + [last], axis=0)
                    if i:
                        tile = pltpu.roll(tile, 128 - 32 * i, 1)
                    tiles.append(tile)
                for i in range(3):
                    high, low = split(jnp.where(lane96 < 96 - 32 * i, tiles[i], tiles[i + 1]))
                    lanes = pl.ds((group * 3 + i) * 128, 128)
                    b_high[column, target, lanes] = high
                    b_low[column, target, lanes] = low

    def product(column, rows):
        a_high, a_low = split(amp[column, rows, :])
        high, low = b_high[column], b_low[column]
        total = jnp.dot(a_high, high, preferred_element_type=jnp.float32)
        total += jnp.dot(a_high, low, preferred_element_type=jnp.float32)
        total += jnp.dot(a_low, high, preferred_element_type=jnp.float32)
        return total

    def multiply(columns, first=False):
        for n, column in enumerate(columns):

            @pl.loop(0, 3)
            def _(m):
                rows = pl.ds(pl.multiple_of(m * 256, 256), 256)
                value = product(column, rows)
                if first and n == 0:
                    out_ref[rows, :] = value
                else:
                    out_ref[rows, :] += value

    for block in blocks.values():
        block[PIECES:] = jnp.zeros((3, PIECE, 128), jnp.float32)

    own_block.wait()
    unpack(0, 0)
    y_step(0)
    for half in halves:
        ring_pass(half, 1, 0)
    for other in (3, 1):
        for half in halves:
            ring_send(half, 2, other)
    y_step(1)
    for half in halves:
        ring_pass(half, 2, 0)
    for key in ((0, 3), (0, 1), (3, 0), (1, 0)):
        unpack(*key)
    y_step(2)
    for half in halves:
        ring_last(half, 1, 0)
    for half in halves:
        ring_send(half, 2, 2)
    y_step(3)
    for half in halves:
        ring_pass(half, 2, 3)
    unpack(3, 3)
    y_step(4)
    for half in halves:
        ring_pass(half, 2, 1)
    for key in ((3, 1), (1, 3), (1, 1)):
        unpack(*key)
    y_step(5)
    for half in halves:
        ring_pass(half, 2, 2)
    y_step(6)
    for half in halves:
        ring_last(half, 2, 0)
    unpack(2, 0)
    unpack(0, 2)
    own_amp.wait()
    shared["own"].wait_recv()
    for half in halves:
        ring_last(half, 2, 3)
    unpack(2, 3)
    unpack(3, 2)
    y_step(7)
    for half in halves:
        ring_last(half, 2, 1)
    unpack(2, 1)
    unpack(1, 2)
    for half in halves:
        ring_last(half, 2, 2)
    unpack(2, 2)

    multiply((col, mate[1]), first=True)
    y_last(0)
    for q in range(CHUNKS):
        shared["below", q].wait_recv()
    multiply((column_of(3, k), column_of(3, 1 - k)))
    y_last(1)
    for q in range(CHUNKS):
        shared["above", q].wait_recv()
    multiply((column_of(1, k), column_of(1, 1 - k)))
    y_last(2)

    def finish(n):
        for q in (up_order[n], down_order[n]):
            shared["far", q].wait_recv()
            rows = rows_of(q)
            out_ref[rows, :] += product(column_of(2, k), rows) + product(column_of(2, 1 - k), rows)

    finish(0)
    finish(1)
    finish(2)
    y_last(3)
    finish(3)
    for copy in started:
        copy.wait_send()


COPIES = 2 * CHUNKS + 1 + CHUNKS + 3 * CHUNKS + 40


def body(amplitudes, integrals, flags):
    packed, table = pl.pallas_call(
        pack_kernel,
        out_shape=(
            jax.ShapeDtypeStruct((PIECES, PIECE, 128), jnp.float32),
            jax.ShapeDtypeStruct((8, 64), jnp.int32),
        ),
        in_specs=[
            pl.BlockSpec(memory_space=pltpu.SMEM),
            pl.BlockSpec(memory_space=pltpu.VMEM),
            pl.BlockSpec(memory_space=pltpu.VMEM),
        ],
        out_specs=(pl.BlockSpec(memory_space=pltpu.VMEM), pl.BlockSpec(memory_space=pltpu.VMEM)),
        scratch_shapes=[pltpu.VMEM((384, 768), jnp.float32)],
        name="pack",
    )(flags, flags, integrals)
    return pl.pallas_call(
        main_kernel,
        out_shape=jax.ShapeDtypeStruct((768, 768), jnp.float32),
        in_specs=[
            pl.BlockSpec(memory_space=pltpu.SMEM),
            pl.BlockSpec(memory_space=pl.ANY),
            pl.BlockSpec(memory_space=pl.ANY),
        ],
        out_specs=pl.BlockSpec(memory_space=pltpu.VMEM),
        scratch_shapes=[
            pltpu.VMEM((8, 768, 768), jnp.float32),
            pltpu.VMEM((8, 768, 768), jnp.bfloat16),
            pltpu.VMEM((8, 768, 768), jnp.bfloat16),
        ]
        + [pltpu.VMEM((PIECES + 3, PIECE, 128), jnp.float32)] * 16
        + [
            pltpu.SemaphoreType.DMA((COPIES,)),
            pltpu.SemaphoreType.DMA((COPIES,)),
            pltpu.SemaphoreType.DMA((2,)),
        ],
        compiler_params=pltpu.CompilerParams(
            collective_id=0, has_side_effects=True, vmem_limit_bytes=66_000_000
        ),
        name="ladder",
    )(table, amplitudes, packed)


def solution(mesh):
    return jax.shard_map(
        body,
        mesh=mesh,
        in_specs=(P("row", "col"), P("col", "row"), P()),
        out_specs=P("row", "col"),
        check_vma=False,
    )
```

time: 290 us -> 115 us (0.40)
  waiting for transfers between devices: 220 us -> 0 us
  Pallas kernels: 0 us -> 111 us
  matrix products: 49.8 us -> 0 us
  between operations: 13.4 us -> 0.01 us
  other arithmetic: 3.17 us -> 0 us
    all_gather x2 -> x0, waiting for transfers between devices: 220 us -> none  [the longest x1 125 us: body(): panel = lax.all_gather(screened, 'row', axis=1, tiled=True)]
    pallas_call x0 -> x2, Pallas kernels: none -> 111 us  [the longest x1 107 us: body(): pl.pallas_call(main_kernel, out_shape=jax.ShapeDtypeStruct((768, 768), jn...]
    dot_general x1 -> x0, matrix products: 49.8 us -> none  [body(): lax.dot_general(lax.all_gather(amplitudes, 'col', axis=1, tiled=True), pa...]
    unnamed x0 -> x1, local copies, waits for them, and re-layouts: none -> 3.22 us
  transfers between devices with their start and end apart: 2 -> 0, of which waited for: 2 -> 0; matrix products, arithmetic and copies ran while one was open for 1% -> 0% of each run, Pallas kernels for 0% -> 0%
where the time goes in v1:
time: 115 us
  Pallas kernels  111 us (97%)
  local copies, waits for them, and re-layouts  3.22 us (3%)
    pallas_call x1, Pallas kernels, body(): pl.pallas_call(main_kernel, out_shape=jax.ShapeDtypeStruct((768, 768), jn...  107 us
    pallas_call x1, Pallas kernels, body(): pl.pallas_call(pack_kernel, out_shape=(jax.ShapeDtypeStruct((PIECES, PIEC...  4.64 us
    unnamed x1, local copies, waits for them, and re-layouts  3.22 us

profile of v1, /device:TPU:1, one launch (start us, length us, event | category | flops | bytes accessed | tf_op | source)
XLA Modules:
  0.0 114.7 jit_solution(3035384855504056766)
XLA Ops:
  0.0 4.6 %pack.1 = (f32[57,24,128]{2,1,0:T(8,128)}, s32[8,64]{1,0:T(8,128)}) custom-call(s32[64,64]{1,0:T(8,128)} %flags_ref.1, s32[64,64]{1,0:T(8,128)} %flags_ref.1, f32[768,384]{1,0:T(8,128)} %x_ref.1), custom_call_target="tpu_custom_call" | custom-call | tf_op jit(solution)/shard_map/pack/pallas_call | solution.py:328
  4.6 106.8 %ladder.1 = f32[768,768]{1,0:T(8,128)} custom-call(s32[8,64]{1,0:T(8,128)} %get-tuple-element.7.table, f32[768,768]{1,0:T(8,128)} %amp_hbm.1, f32[57,24,128]{2,1,0:T(8,128)} %get-tuple-element.8.packed_hbm), custom_call_target="tpu_custom_call" | custom-call | tf_op jit(solution)/shard_map/ladder/pallas_call | solution.py:343
  111.5 3.2 %copy.5 = f32[768,768]{1,0:T(8,128)} copy(f32[768,768]{1,0:T(8,128)} %ladder.1) | data formatting | bytes 4718592

commit v2 on v1

--- a/solution.py
+++ b/solution.py
@@ -222,28 +222,31 @@
                     b_high[column, target, lanes] = high
                     b_low[column, target, lanes] = low
 
-    def product(column, rows):
-        a_high, a_low = split(amp[column, rows, :])
+    def product(column, left):
+        a_high, a_low = split(left)
         high, low = b_high[column], b_low[column]
-        total = jnp.dot(a_high, high, preferred_element_type=jnp.float32)
-        total += jnp.dot(a_high, low, preferred_element_type=jnp.float32)
-        total += jnp.dot(a_low, high, preferred_element_type=jnp.float32)
-        return total
-
-    def multiply(columns, first=False):
-        for n, column in enumerate(columns):
-
-            @pl.loop(0, 3)
-            def _(m):
-                rows = pl.ds(pl.multiple_of(m * 256, 256), 256)
-                value = product(column, rows)
-                if first and n == 0:
-                    out_ref[rows, :] = value
-                else:
-                    out_ref[rows, :] += value
+        return jnp.dot(
+            jnp.concatenate([a_high, a_high, a_low], axis=1),
+            jnp.concatenate([high, low, high], axis=0),
+            preferred_element_type=jnp.float32,
+        )
+
+    near = lax.div(x, 2)
+
+    def multiply(dz, core, half, wanted):
+        zs = lax.rem(z + dz, 4)
+        dy = lax.rem(zs + 4 - y, 4)
+        first = (dy == 0) | ((dy == 3) & (half == 0)) | ((dy == 1) & (half == 1))
+
+        @pl.when(wanted(dy, first))
+        def _():
+            rows = pl.ds(pl.multiple_of(half * 384, 384), 384)
+            column = zs * 2 + core
+            out_ref[rows, :] += product(column, amp[column, rows, :])
 
     for block in blocks.values():
         block[PIECES:] = jnp.zeros((3, PIECE, 128), jnp.float32)
+    out_ref[...] = jnp.zeros_like(out_ref)
 
     own_block.wait()
     unpack(0, 0)
@@ -272,6 +275,16 @@
         ring_pass(half, 2, 1)
     for key in ((3, 1), (1, 3), (1, 1)):
         unpack(*key)
+    own_amp.wait()
+    shared["own"].wait_recv()
+    for q in range(4):
+        shared["below", q].wait_recv()
+        shared["above", q + 4].wait_recv()
+
+    @pl.loop(0, 6)
+    def _(n):
+        multiply(lax.rem(3 + lax.div(n, 2), 4), near, lax.rem(n, 2), lambda dy, first: first)
+
     y_step(5)
     for half in halves:
         ring_pass(half, 2, 2)
@@ -280,8 +293,6 @@
         ring_last(half, 2, 0)
     unpack(2, 0)
     unpack(0, 2)
-    own_amp.wait()
-    shared["own"].wait_recv()
     for half in halves:
         ring_last(half, 2, 3)
     unpack(2, 3)
@@ -291,32 +302,50 @@
         ring_last(half, 2, 1)
     unpack(2, 1)
     unpack(1, 2)
+    for q in range(4):
+        shared["below", q + 4].wait_recv()
+        shared["above", q].wait_recv()
+
+    @pl.loop(0, 14)
+    def _(n):
+        entry = lax.div(n, 2)
+        done = entry < 3
+        core = jnp.where(entry < 4, near, 1 - near)
+        multiply(
+            lax.rem(3 + entry, 4), core, lax.rem(n, 2),
+            lambda dy, first: (dy != 2) & jnp.logical_not(done & first))
+
+    y_last(0)
     for half in halves:
         ring_last(half, 2, 2)
     unpack(2, 2)
 
-    multiply((col, mate[1]), first=True)
-    y_last(0)
-    for q in range(CHUNKS):
-        shared["below", q].wait_recv()
-    multiply((column_of(3, k), column_of(3, 1 - k)))
-    y_last(1)
-    for q in range(CHUNKS):
-        shared["above", q].wait_recv()
-    multiply((column_of(1, k), column_of(1, 1 - k)))
-    y_last(2)
-
-    def finish(n):
+    @pl.loop(0, 2)
+    def _(n):
+        multiply(jnp.int32(2), 1 - near, n, lambda dy, first: dy != 2)
+
+    def finish(n, column):
+        rows = [rows_of(q) for q in (up_order[n], down_order[n])]
+        value = product(column, jnp.concatenate([amp[column, r, :] for r in rows], axis=0))
+        out_ref[rows[0], :] += value[:CHUNK]
+        out_ref[rows[1], :] += value[CHUNK:]
+
+    def finish_shared(n):
         for q in (up_order[n], down_order[n]):
             shared["far", q].wait_recv()
-            rows = rows_of(q)
-            out_ref[rows, :] += product(column_of(2, k), rows) + product(column_of(2, 1 - k), rows)
-
-    finish(0)
-    finish(1)
-    finish(2)
+        finish(n, column_of(2, 1 - k))
+
+    y_last(1)
+    finish(0, column_of(2, k))
+    finish_shared(0)
+    finish(1, column_of(2, k))
+    y_last(2)
+    finish_shared(1)
+    finish(2, column_of(2, k))
     y_last(3)
-    finish(3)
+    finish_shared(2)
+    finish(3, column_of(2, k))
+    finish_shared(3)
     for copy in started:
         copy.wait_send()
 

time: 115 us -> 99.2 us (0.86)
  Pallas kernels: 111 us -> 95.2 us
    pallas_call x1, Pallas kernels: 107 us -> 90.6 us  [body(): pl.pallas_call(main_kernel, out_shape=jax.ShapeDtypeStruct((768, 768), jn...]
where the time goes in v2:
time: 99.2 us; the launch traced here: 98.5 us
  Pallas kernels  95.2 us (96%)
  local copies, waits for them, and re-layouts  3.22 us (3%)
    pallas_call x1, Pallas kernels, body(): pl.pallas_call(main_kernel, out_shape=jax.ShapeDtypeStruct((768, 768), jn...  90.6 us
    pallas_call x1, Pallas kernels, body(): pl.pallas_call(pack_kernel, out_shape=(jax.ShapeDtypeStruct((PIECES, PIEC...  4.57 us
    unnamed x1, local copies, waits for them, and re-layouts  3.22 us

profile of v2, /device:TPU:1, one launch (start us, length us, event | category | flops | bytes accessed | tf_op | source)
XLA Modules:
  0.0 98.5 jit_solution(6758625843529854174)
XLA Ops:
  0.0 4.6 %pack.1 = (f32[57,24,128]{2,1,0:T(8,128)}, s32[8,64]{1,0:T(8,128)}) custom-call(s32[64,64]{1,0:T(8,128)} %flags_ref.1, s32[64,64]{1,0:T(8,128)} %flags_ref.1, f32[768,384]{1,0:T(8,128)} %x_ref.1), custom_call_target="tpu_custom_call" | custom-call | tf_op jit(solution)/shard_map/pack/pallas_call | solution.py:357
  4.6 90.6 %ladder.1 = f32[768,768]{1,0:T(8,128)} custom-call(s32[8,64]{1,0:T(8,128)} %get-tuple-element.7.table, f32[768,768]{1,0:T(8,128)} %amp_hbm.1, f32[57,24,128]{2,1,0:T(8,128)} %get-tuple-element.8.packed_hbm), custom_call_target="tpu_custom_call" | custom-call | tf_op jit(solution)/shard_map/ladder/pallas_call | solution.py:372
  95.2 3.2 %copy.5 = f32[768,768]{1,0:T(8,128)} copy(f32[768,768]{1,0:T(8,128)} %ladder.1) | data formatting | bytes 4718592

commit v3 on v2

--- a/solution.py
+++ b/solution.py
@@ -22,53 +22,13 @@
     return lax.broadcasted_iota(jnp.int32, (rows, 128), 1)
 
 
-def pack_kernel(flags_smem, flags_ref, x_ref, packed_ref, table_ref, turned):
-    row, col = lax.axis_index("row"), lax.axis_index("col")
-    own = flags_ref[pl.ds(pl.multiple_of(col * 8, 8), 8), :].astype(jnp.float32)
-    d_from = lax.broadcasted_iota(jnp.int32, (64, 64), 0)
-    d_to = lax.broadcasted_iota(jnp.int32, (64, 64), 1)
-    earlier = ((d_from // 4 == d_to // 4) & (d_from < d_to)).astype(jnp.float32)
-    i_to = lax.broadcasted_iota(jnp.int32, (8, 8), 0)
-    i_from = lax.broadcasted_iota(jnp.int32, (8, 8), 1)
-    above = (i_from < i_to).astype(jnp.float32)
-    before = jnp.dot(own, earlier, preferred_element_type=jnp.float32)
-    rank = jnp.dot(above, own, preferred_element_type=jnp.float32) + jnp.sum(before, axis=0, keepdims=True)
-    table_ref[...] = (jnp.where(own > 0.5, rank, float(CAP)) * 3.0).astype(jnp.int32)
-
-    packed_ref[...] = jnp.zeros_like(packed_ref)
-    turned[...] = x_ref[...].T
-    lane = lanes_of(TILE)
-    count = jnp.int32(0)
-    for j in range(4):
-        for i in range(8):
-            flag = flags_smem[col * 8 + i, row * 4 + j]
-
-            @pl.when(flag != 0)
-            def _():
-                rows = slice(j * TILE, (j + 1) * TILE)
-                first, offset = divmod(i * TILE, 128)
-                tile = turned[rows, first * 128 : first * 128 + 128]
-                if offset:
-                    tile = pltpu.roll(tile, 128 - offset, 1)
-                if offset > 32:
-                    right = pltpu.roll(turned[rows, first * 128 + 128 : first * 128 + 256], 128 - offset, 1)
-                    tile = jnp.where(lane < 128 - offset, tile, right)
-                last = tile[3 * PIECE :]
-                for q in range(3):
-                    piece = tile[q * PIECE : (q + 1) * PIECE]
-                    packed_ref[3 * count + q] = jnp.where(
-                        lanes_of(PIECE) < TILE, piece, pltpu.roll(last, 96 - 32 * q, 1))
-
-            count = count + flag
-
-
 def split(value):
     high = value.astype(jnp.bfloat16)
     low = (value - high.astype(jnp.float32)).astype(jnp.bfloat16)
     return high, low
 
 
-def main_kernel(table, amp_hbm, packed_hbm, out_ref, amp, b_high, b_low, *rest):
+def main_kernel(flags, amp_hbm, x_hbm, out_ref, amp, b_high, b_low, x_ref, turned, tiles, table, *rest):
     blocks = {(dx, dz): rest[dx * 4 + dz] for dx in range(4) for dz in range(4)}
     send_sem, recv_sem, local_sem = rest[16:]
     row, col = lax.axis_index("row"), lax.axis_index("col")
@@ -88,6 +48,11 @@
 
     def column_of(d, core):
         return lax.rem(y + d, 4) * 2 + core
+
+    own_x = pltpu.make_async_copy(x_hbm, x_ref, local_sem.at[1])
+    own_x.start()
+    own_amp = pltpu.make_async_copy(amp_hbm, amp.at[col], local_sem.at[0])
+    own_amp.start()
 
     barrier = pltpu.get_barrier_semaphore()
     for peer in (at_x(1), at_x(3), at_z(1), at_z(3), at_y(1), at_y(3), mate):
@@ -131,8 +96,7 @@
         return at_x(d) if (half is FIRST) == (phase == 1) else at_z(d)
 
     def ring_send(half, phase, other):
-        own = key_of(half, phase, other, 0)
-        src = packed_hbm if own == (0, 0) else blocks[own]
+        src = blocks[key_of(half, phase, other, 0)]
         ring[half, phase, other, "up"] = send(
             part(src, half), part(blocks[key_of(half, phase, other, 3)], half), peer_of(half, phase, 1))
         ring[half, phase, other, "down"] = send(
@@ -155,16 +119,7 @@
 
     halves = (FIRST, SECOND)
 
-    send_own(0)
-    for half in halves:
-        ring_send(half, 1, 0)
-    for half in halves:
-        ring_send(half, 2, 0)
-    own_amp = pltpu.make_async_copy(amp_hbm, amp.at[col], local_sem.at[0])
-    own_amp.start()
-    own_block = pltpu.make_async_copy(packed_hbm, blocks[0, 0].at[pl.ds(0, PIECES)], local_sem.at[1])
-    own_block.start()
-    for n in range(1, CHUNKS):
+    for n in range(CHUNKS):
         send_own(n)
     shared["own"] = send(amp_hbm, amp.at[col], mate)
 
@@ -193,6 +148,42 @@
         pass_down[q].wait_recv()
         share(("far", q), far, q)
 
+    def locate(source):
+        count = jnp.int32(0)
+        for j in range(4):
+            for i in range(8):
+                flag = flags[col * 8 + i, source * 4 + j]
+                table[i, source * 4 + j] = PIECES + flag * (3 * count - PIECES)
+                count = count + flag
+
+    def pack():
+        turned[...] = x_ref[...].T
+        lane, short = lanes_of(TILE), lanes_of(PIECE)
+        for j in range(4):
+            rows = slice(j * TILE, (j + 1) * TILE)
+            for i in range(8):
+                first, offset = divmod(i * TILE, 128)
+                tile = turned[rows, first * 128 : first * 128 + 128]
+                if offset > 32:
+                    right = turned[rows, first * 128 + 128 : first * 128 + 256]
+                    tile = jnp.where(lane < offset, right, tile)
+                spare = (offset + 96) % 128
+                free = (short >= spare) & (short < spare + 32)
+                last = tile[3 * PIECE :]
+                for q in range(3):
+                    piece = tile[q * PIECE : (q + 1) * PIECE]
+                    tiles[3 * (8 * j + i) + q] = jnp.where(free, pltpu.roll(last, 96 - 32 * q, 1), piece)
+
+        @pl.loop(0, CAP)
+        def _(t):
+            chosen = jnp.int32(0)
+            for j in range(4):
+                for i in range(8):
+                    away = table[i, row * 4 + j] - 3 * t
+                    chosen = chosen + (8 * j + i) * (1 - jnp.minimum(jnp.maximum(away, -away), 1))
+            for q in range(3):
+                blocks[0, 0][3 * t + q] = tiles[3 * chosen + q]
+
     lane24, lane96 = lanes_of(PIECE), lanes_of(TILE)
 
     def unpack(dx, dz):
@@ -206,18 +197,16 @@
         def _(j):
             target = pl.ds(pl.multiple_of(base + j * TILE, 32), TILE)
             for group in range(2):
-                tiles = []
+                parts = []
                 for i in range(4):
                     start = table[group * 4 + i, source * 4 + j]
                     pieces = [block[start + q] for q in range(3)]
-                    turned = [pltpu.roll(pieces[q], 32 + 32 * q, 1) for q in range(3)]
-                    last = jnp.where(lane24 < 32, turned[0], jnp.where(lane24 < 64, turned[1], turned[2]))
-                    tile = jnp.concatenate(pieces + [last], axis=0)
-                    if i:
-                        tile = pltpu.roll(tile, 128 - 32 * i, 1)
-                    tiles.append(tile)
+                    moved = [pltpu.roll(pieces[q], 32 + 32 * q, 1) for q in range(3)]
+                    part_of = [(lane24 >= (q - i) % 4 * 32) & (lane24 < (q - i) % 4 * 32 + 32) for q in range(2)]
+                    last = jnp.where(part_of[0], moved[0], jnp.where(part_of[1], moved[1], moved[2]))
+                    parts.append(jnp.concatenate(pieces + [last], axis=0))
                 for i in range(3):
-                    high, low = split(jnp.where(lane96 < 96 - 32 * i, tiles[i], tiles[i + 1]))
+                    high, low = split(jnp.where(lane96 < 96 - 32 * i, parts[i], parts[i + 1]))
                     lanes = pl.ds((group * 3 + i) * 128, 128)
                     b_high[column, target, lanes] = high
                     b_low[column, target, lanes] = low
@@ -244,11 +233,22 @@
             column = zs * 2 + core
             out_ref[rows, :] += product(column, amp[column, rows, :])
 
+    locate(row)
+    own_x.wait()
+    pack()
     for block in blocks.values():
         block[PIECES:] = jnp.zeros((3, PIECE, 128), jnp.float32)
     out_ref[...] = jnp.zeros_like(out_ref)
 
-    own_block.wait()
+    for half in halves:
+        ring_send(half, 1, 0)
+    for half in halves:
+        ring_send(half, 2, 0)
+
+    @pl.loop(0, 16)
+    def _(source):
+        locate(source)
+
     unpack(0, 0)
     y_step(0)
     for half in halves:
@@ -275,6 +275,7 @@
         ring_pass(half, 2, 1)
     for key in ((3, 1), (1, 3), (1, 1)):
         unpack(*key)
+    y_step(5)
     own_amp.wait()
     shared["own"].wait_recv()
     for q in range(4):
@@ -285,7 +286,6 @@
     def _(n):
         multiply(lax.rem(3 + lax.div(n, 2), 4), near, lax.rem(n, 2), lambda dy, first: first)
 
-    y_step(5)
     for half in halves:
         ring_pass(half, 2, 2)
     y_step(6)
@@ -293,59 +293,64 @@
         ring_last(half, 2, 0)
     unpack(2, 0)
     unpack(0, 2)
+    y_step(7)
     for half in halves:
         ring_last(half, 2, 3)
     unpack(2, 3)
     unpack(3, 2)
-    y_step(7)
+    for q in range(4):
+        shared["below", q + 4].wait_recv()
+        shared["above", q].wait_recv()
+
+    @pl.loop(0, 10)
+    def _(n):
+        entry = lax.div(n, 2)
+        done = entry < 3
+        core = jnp.where(entry < 3, near, 1 - near)
+        multiply(
+            lax.rem(3 + lax.rem(entry, 3), 4), core, lax.rem(n, 2),
+            lambda dy, first: (dy != 2) & jnp.logical_not(done & first))
+
     for half in halves:
         ring_last(half, 2, 1)
     unpack(2, 1)
     unpack(1, 2)
-    for q in range(4):
-        shared["below", q + 4].wait_recv()
-        shared["above", q].wait_recv()
-
-    @pl.loop(0, 14)
+    y_last(0)
+
+    @pl.loop(0, 4)
     def _(n):
         entry = lax.div(n, 2)
-        done = entry < 3
-        core = jnp.where(entry < 4, near, 1 - near)
-        multiply(
-            lax.rem(3 + entry, 4), core, lax.rem(n, 2),
-            lambda dy, first: (dy != 2) & jnp.logical_not(done & first))
-
-    y_last(0)
+        core = jnp.where(entry == 0, near, 1 - near)
+        multiply(2 - entry, core, lax.rem(n, 2), lambda dy, first: dy != 2)
+
     for half in halves:
         ring_last(half, 2, 2)
     unpack(2, 2)
+    y_last(1)
 
     @pl.loop(0, 2)
     def _(n):
         multiply(jnp.int32(2), 1 - near, n, lambda dy, first: dy != 2)
 
-    def finish(n, column):
-        rows = [rows_of(q) for q in (up_order[n], down_order[n])]
+    def finish(since, until, column):
+        size = (until - since) * CHUNK
+        rows = [pl.ds(order[since] * CHUNK, size) for order in (up_order, down_order)]
         value = product(column, jnp.concatenate([amp[column, r, :] for r in rows], axis=0))
-        out_ref[rows[0], :] += value[:CHUNK]
-        out_ref[rows[1], :] += value[CHUNK:]
-
-    def finish_shared(n):
-        for q in (up_order[n], down_order[n]):
-            shared["far", q].wait_recv()
-        finish(n, column_of(2, 1 - k))
-
-    y_last(1)
-    finish(0, column_of(2, k))
-    finish_shared(0)
-    finish(1, column_of(2, k))
+        out_ref[rows[0], :] += value[:size]
+        out_ref[rows[1], :] += value[size:]
+
+    def finish_shared(since, until):
+        for n in range(since, until):
+            for q in (up_order[n], down_order[n]):
+                shared["far", q].wait_recv()
+        finish(since, until, column_of(2, 1 - k))
+
     y_last(2)
-    finish_shared(1)
-    finish(2, column_of(2, k))
+    finish(0, 3, column_of(2, k))
+    finish_shared(0, 3)
     y_last(3)
-    finish_shared(2)
-    finish(3, column_of(2, k))
-    finish_shared(3)
+    finish(3, 4, column_of(2, k))
+    finish_shared(3, 4)
     for copy in started:
         copy.wait_send()
 
@@ -354,24 +359,9 @@
 
 
 def body(amplitudes, integrals, flags):
-    packed, table = pl.pallas_call(
-        pack_kernel,
-        out_shape=(
-            jax.ShapeDtypeStruct((PIECES, PIECE, 128), jnp.float32),
-            jax.ShapeDtypeStruct((8, 64), jnp.int32),
-        ),
-        in_specs=[
-            pl.BlockSpec(memory_space=pltpu.SMEM),
-            pl.BlockSpec(memory_space=pltpu.VMEM),
-            pl.BlockSpec(memory_space=pltpu.VMEM),
-        ],
-        out_specs=(pl.BlockSpec(memory_space=pltpu.VMEM), pl.BlockSpec(memory_space=pltpu.VMEM)),
-        scratch_shapes=[pltpu.VMEM((384, 768), jnp.float32)],
-        name="pack",
-    )(flags, flags, integrals)
     return pl.pallas_call(
         main_kernel,
-        out_shape=jax.ShapeDtypeStruct((768, 768), jnp.float32),
+        out_shape=pltpu.VMEM((768, 768), jnp.float32),
         in_specs=[
             pl.BlockSpec(memory_space=pltpu.SMEM),
             pl.BlockSpec(memory_space=pl.ANY),
@@ -382,6 +372,10 @@
             pltpu.VMEM((8, 768, 768), jnp.float32),
             pltpu.VMEM((8, 768, 768), jnp.bfloat16),
             pltpu.VMEM((8, 768, 768), jnp.bfloat16),
+            pltpu.VMEM((768, 384), jnp.float32),
+            pltpu.VMEM((384, 768), jnp.float32),
+            pltpu.VMEM((96, PIECE, 128), jnp.float32),
+            pltpu.SMEM((8, 64), jnp.int32),
         ]
         + [pltpu.VMEM((PIECES + 3, PIECE, 128), jnp.float32)] * 16
         + [
@@ -390,10 +384,10 @@
             pltpu.SemaphoreType.DMA((2,)),
         ],
         compiler_params=pltpu.CompilerParams(
-            collective_id=0, has_side_effects=True, vmem_limit_bytes=66_000_000
+            collective_id=0, has_side_effects=True, vmem_limit_bytes=62_000_000
         ),
         name="ladder",
-    )(table, amplitudes, packed)
+    )(flags, amplitudes, integrals)
 
 
 def solution(mesh):

time: 99.2 us -> 93.3 us (0.941)
  Pallas kernels: 95.2 us -> 91.6 us
  local copies, waits for them, and re-layouts: 3.22 us -> 1.41 us
    pallas_call x2 -> x1, Pallas kernels: 95.2 us -> 91.6 us  [body(): pl.pallas_call(main_kernel, out_shape=pltpu.VMEM((768, 768), jnp.float32)...]
    unnamed x1, local copies, waits for them, and re-layouts: 3.22 us -> 1.41 us
where the time goes in v3:
time: 93.3 us; the launch traced here: 93.1 us
  Pallas kernels  91.6 us (98%)
  local copies, waits for them, and re-layouts  1.41 us (2%)
    pallas_call x1, Pallas kernels, body(): pl.pallas_call(main_kernel, out_shape=pltpu.VMEM((768, 768), jnp.float32)...  91.6 us

profile of v3, /device:TPU:1, one launch (start us, length us, event | category | flops | bytes accessed | tf_op | source)
XLA Modules:
  0.0 93.1 jit_solution(7372423844396035313)
XLA Ops:
  0.0 91.6 %ladder.1 = f32[768,768]{1,0:T(8,128)S(1)} custom-call(s32[64,64]{1,0:T(8,128)} %flags.1, f32[768,768]{1,0:T(8,128)} %amp_hbm.1, f32[768,384]{1,0:T(8,128)} %x_hbm.1), custom_call_target="tpu_custom_call" | custom-call | tf_op jit(solution)/shard_map/ladder/pallas_call | solution.py:362
  91.7 1.4 %copy.5 = f32[768,768]{1,0:T(8,128)} copy(f32[768,768]{1,0:T(8,128)S(1)} %ladder.1) | data formatting | bytes 4718592

commit v4 on v3

--- a/solution.py
+++ b/solution.py
@@ -10,8 +10,8 @@
 PIECE = 24
 PIECES = 3 * CAP
 MESH = pl.DeviceIdType.MESH
-CHUNKS = 8
-CHUNK = 96
+STARTS = (0, 224, 336, 384, 608, 720, 768)
+CHUNKS = 6
 
 FIRST, SECOND = (0, 29), (29, 28)
 PASS_UP = {FIRST: (0, 14), SECOND: (29, 14)}
@@ -28,7 +28,7 @@
     return high, low
 
 
-def main_kernel(flags, amp_hbm, x_hbm, out_ref, amp, b_high, b_low, x_ref, turned, tiles, table, *rest):
+def main_kernel(flags_hbm, amp_hbm, x_hbm, out_ref, amp, b_high, b_low, x_ref, turned, tiles, flags, table, *rest):
     blocks = {(dx, dz): rest[dx * 4 + dz] for dx in range(4) for dz in range(4)}
     send_sem, recv_sem, local_sem = rest[16:]
     row, col = lax.axis_index("row"), lax.axis_index("col")
@@ -49,6 +49,8 @@
     def column_of(d, core):
         return lax.rem(y + d, 4) * 2 + core
 
+    own_flags = pltpu.make_async_copy(flags_hbm, flags, local_sem.at[2])
+    own_flags.start()
     own_x = pltpu.make_async_copy(x_hbm, x_ref, local_sem.at[1])
     own_x.start()
     own_amp = pltpu.make_async_copy(amp_hbm, amp.at[col], local_sem.at[0])
@@ -72,10 +74,10 @@
         return copy
 
     def rows_of(q):
-        return pl.ds(q * CHUNK, CHUNK)
+        return pl.ds(STARTS[q], STARTS[q + 1] - STARTS[q])
 
     up, down, pass_up, pass_down, shared = {}, {}, {}, {}, {}
-    up_order, down_order = (0, 1, 2, 3, 4, 5, 6, 7), (4, 5, 6, 7, 0, 1, 2, 3)
+    up_order, down_order = (0, 1, 2, 3, 4, 5), (3, 4, 5, 0, 1, 2)
 
     def send_own(n):
         q = up_order[n]
@@ -130,12 +132,12 @@
         below, above = column_of(3, k), column_of(1, k)
         q = up_order[n]
         up[q].wait_recv()
-        if n < 4:
+        if n < 3:
             pass_up[q] = send(amp.at[below, rows_of(q)], amp.at[below, rows_of(q)], at_y(1))
         share(("below", q), below, q)
         q = down_order[n]
         down[q].wait_recv()
-        if n < 4:
+        if n < 3:
             pass_down[q] = send(amp.at[above, rows_of(q)], amp.at[above, rows_of(q)], at_y(3))
         share(("above", q), above, q)
 
@@ -211,9 +213,9 @@
                     b_high[column, target, lanes] = high
                     b_low[column, target, lanes] = low
 
-    def product(column, left):
+    def product(column, left, depth=slice(None)):
         a_high, a_low = split(left)
-        high, low = b_high[column], b_low[column]
+        high, low = b_high[column, depth, :], b_low[column, depth, :]
         return jnp.dot(
             jnp.concatenate([a_high, a_high, a_low], axis=1),
             jnp.concatenate([high, low, high], axis=0),
@@ -221,18 +223,35 @@
         )
 
     near = lax.div(x, 2)
-
-    def multiply(dz, core, half, wanted):
+    far = 1 - near
+    same = pl.ds(pl.multiple_of(lax.rem(x, 2) * 384, 128), 384)
+    other_block = pl.ds(pl.multiple_of((1 - lax.rem(x, 2)) * 384, 128), 384)
+
+    def multiply(dz, core, half, whole=None, block=None, partly=None):
         zs = lax.rem(z + dz, 4)
         dy = lax.rem(zs + 4 - y, 4)
         first = (dy == 0) | ((dy == 3) & (half == 0)) | ((dy == 1) & (half == 1))
-
-        @pl.when(wanted(dy, first))
-        def _():
-            rows = pl.ds(pl.multiple_of(half * 384, 384), 384)
-            column = zs * 2 + core
-            out_ref[rows, :] += product(column, amp[column, rows, :])
-
+        rows = pl.ds(pl.multiple_of(half * 384, 384), 384)
+        column = zs * 2 + core
+        if whole is not None:
+
+            @pl.when(whole(dy, first))
+            def _():
+                out_ref[rows, :] += product(column, amp[column, rows, :])
+
+        if block is not None:
+
+            @pl.when(partly(dy, first))
+            def _():
+                out_ref[rows, :] += product(column, amp[column, rows, block], block)
+
+    def early(dy, first):
+        return first
+
+    def late(dy, first):
+        return (dy != 2) & jnp.logical_not(first)
+
+    own_flags.wait()
     locate(row)
     own_x.wait()
     pack()
@@ -250,107 +269,122 @@
         locate(source)
 
     unpack(0, 0)
-    y_step(0)
     for half in halves:
         ring_pass(half, 1, 0)
     for other in (3, 1):
         for half in halves:
             ring_send(half, 2, other)
-    y_step(1)
+    y_step(0)
     for half in halves:
         ring_pass(half, 2, 0)
     for key in ((0, 3), (0, 1), (3, 0), (1, 0)):
         unpack(*key)
+    for half in halves:
+        ring_last(half, 1, 0)
+    for half in halves:
+        ring_send(half, 2, 2)
+    y_step(1)
     y_step(2)
-    for half in halves:
-        ring_last(half, 1, 0)
-    for half in halves:
-        ring_send(half, 2, 2)
-    y_step(3)
     for half in halves:
         ring_pass(half, 2, 3)
     unpack(3, 3)
-    y_step(4)
     for half in halves:
         ring_pass(half, 2, 1)
     for key in ((3, 1), (1, 3), (1, 1)):
         unpack(*key)
-    y_step(5)
+    y_step(3)
     own_amp.wait()
     shared["own"].wait_recv()
-    for q in range(4):
+    for q in range(3):
         shared["below", q].wait_recv()
-        shared["above", q + 4].wait_recv()
+        shared["above", q + 3].wait_recv()
 
     @pl.loop(0, 6)
     def _(n):
-        multiply(lax.rem(3 + lax.div(n, 2), 4), near, lax.rem(n, 2), lambda dy, first: first)
+        multiply(lax.rem(3 + lax.div(n, 2), 4), near, lax.rem(n, 2), early)
 
     for half in halves:
         ring_pass(half, 2, 2)
-    y_step(6)
+    y_step(4)
+
+    @pl.loop(0, 6)
+    def _(n):
+        multiply(lax.rem(3 + lax.div(n, 2), 4), far, lax.rem(n, 2), None, other_block, early)
+
     for half in halves:
         ring_last(half, 2, 0)
     unpack(2, 0)
     unpack(0, 2)
-    y_step(7)
+
+    @pl.loop(0, 4)
+    def _(n):
+        entry = lax.div(n, 2)
+        multiply(2 * entry, jnp.where(entry == 0, far, near), lax.rem(n, 2), None, same, early)
+
+    y_step(5)
     for half in halves:
         ring_last(half, 2, 3)
     unpack(2, 3)
     unpack(3, 2)
-    for q in range(4):
-        shared["below", q + 4].wait_recv()
+    for q in range(3):
+        shared["below", q + 3].wait_recv()
         shared["above", q].wait_recv()
 
-    @pl.loop(0, 10)
+    @pl.loop(0, 8)
     def _(n):
         entry = lax.div(n, 2)
-        done = entry < 3
-        core = jnp.where(entry < 3, near, 1 - near)
-        multiply(
-            lax.rem(3 + lax.rem(entry, 3), 4), core, lax.rem(n, 2),
-            lambda dy, first: (dy != 2) & jnp.logical_not(done & first))
+        core = jnp.where(entry < 3, near, far)
+        multiply(lax.rem(3 + entry, 4) * jnp.where(entry < 3, 1, 0), core, lax.rem(n, 2), late)
+
+    @pl.loop(0, 2)
+    def _(n):
+        multiply(jnp.int32(3), far, n, late, same, early)
 
     for half in halves:
         ring_last(half, 2, 1)
     unpack(2, 1)
     unpack(1, 2)
-    y_last(0)
 
     @pl.loop(0, 4)
     def _(n):
         entry = lax.div(n, 2)
-        core = jnp.where(entry == 0, near, 1 - near)
-        multiply(2 - entry, core, lax.rem(n, 2), lambda dy, first: dy != 2)
+        core = jnp.where(entry == 0, near, far)
+        block = pl.ds(pl.multiple_of(jnp.where(entry == 0, other_block.start, same.start), 128), 384)
+        multiply(2 - entry, core, lax.rem(n, 2), late, block, early)
 
     for half in halves:
         ring_last(half, 2, 2)
     unpack(2, 2)
-    y_last(1)
+    y_last(0)
 
     @pl.loop(0, 2)
     def _(n):
         multiply(jnp.int32(2), 1 - near, n, lambda dy, first: dy != 2)
 
-    def finish(since, until, column):
-        size = (until - since) * CHUNK
-        rows = [pl.ds(order[since] * CHUNK, size) for order in (up_order, down_order)]
-        value = product(column, jnp.concatenate([amp[column, r, :] for r in rows], axis=0))
+    def finish(n, column):
+        rows = [rows_of(q) for q in (up_order[n], down_order[n])]
+        size = rows[0].size
+        a_high, a_low = split(jnp.concatenate([amp[column, r, :] for r in rows], axis=0))
+        value = jnp.dot(
+            jnp.concatenate([a_high, a_low], axis=0), b_high[column], preferred_element_type=jnp.float32)
+        value = value[: 2 * size] + value[2 * size :]
+        value += jnp.dot(a_high, b_low[column], preferred_element_type=jnp.float32)
         out_ref[rows[0], :] += value[:size]
         out_ref[rows[1], :] += value[size:]
 
-    def finish_shared(since, until):
-        for n in range(since, until):
-            for q in (up_order[n], down_order[n]):
-                shared["far", q].wait_recv()
-        finish(since, until, column_of(2, 1 - k))
-
+    def finish_shared(n):
+        for q in (up_order[n], down_order[n]):
+            shared["far", q].wait_recv()
+        finish(n, column_of(2, 1 - k))
+
+    finish(0, column_of(2, k))
+    y_last(1)
+    finish_shared(0)
+    finish(1, column_of(2, k))
     y_last(2)
-    finish(0, 3, column_of(2, k))
-    finish_shared(0, 3)
-    y_last(3)
-    finish(3, 4, column_of(2, k))
-    finish_shared(3, 4)
+    finish_shared(1)
+    finish(2, column_of(2, k))
+    finish_shared(2)
     for copy in started:
         copy.wait_send()
 
@@ -363,7 +397,7 @@
         main_kernel,
         out_shape=pltpu.VMEM((768, 768), jnp.float32),
         in_specs=[
-            pl.BlockSpec(memory_space=pltpu.SMEM),
+            pl.BlockSpec(memory_space=pl.ANY),
             pl.BlockSpec(memory_space=pl.ANY),
             pl.BlockSpec(memory_space=pl.ANY),
         ],
@@ -375,13 +409,14 @@
             pltpu.VMEM((768, 384), jnp.float32),
             pltpu.VMEM((384, 768), jnp.float32),
             pltpu.VMEM((96, PIECE, 128), jnp.float32),
+            pltpu.SMEM((64, 64), jnp.int32),
             pltpu.SMEM((8, 64), jnp.int32),
         ]
         + [pltpu.VMEM((PIECES + 3, PIECE, 128), jnp.float32)] * 16
         + [
             pltpu.SemaphoreType.DMA((COPIES,)),
             pltpu.SemaphoreType.DMA((COPIES,)),
-            pltpu.SemaphoreType.DMA((2,)),
+            pltpu.SemaphoreType.DMA((3,)),
         ],
         compiler_params=pltpu.CompilerParams(
             collective_id=0, has_side_effects=True, vmem_limit_bytes=62_000_000

time: 93.3 us -> 90.7 us (0.972)
  Pallas kernels: 91.6 us -> 89.2 us
    pallas_call x1, Pallas kernels: 91.6 us -> 89.2 us  [body(): pl.pallas_call(main_kernel, out_shape=pltpu.VMEM((768, 768), jnp.float32)...]
where the time goes in v4:
time: 90.7 us
  Pallas kernels  89.2 us (98%)
  local copies, waits for them, and re-layouts  1.41 us (2%)
    pallas_call x1, Pallas kernels, body(): pl.pallas_call(main_kernel, out_shape=pltpu.VMEM((768, 768), jnp.float32)...  89.2 us

profile of v4, /device:TPU:1, one launch (start us, length us, event | category | flops | bytes accessed | tf_op | source)
XLA Modules:
  0.0 90.7 jit_solution(14515969846844196231)
XLA Ops:
  0.0 89.2 %ladder.1 = f32[768,768]{1,0:T(8,128)S(1)} custom-call(s32[64,64]{1,0:T(8,128)} %flags_hbm.1, f32[768,768]{1,0:T(8,128)} %amp_hbm.1, f32[768,384]{1,0:T(8,128)} %x_hbm.1), custom_call_target="tpu_custom_call" | custom-call | tf_op jit(solution)/shard_map/ladder/pallas_call | solution.py:396
  89.2 1.4 %copy.5 = f32[768,768]{1,0:T(8,128)} copy(f32[768,768]{1,0:T(8,128)S(1)} %ladder.1) | data formatting | bytes 4718592

commit v5 on v4

--- a/solution.py
+++ b/solution.py
@@ -10,7 +10,7 @@
 PIECE = 24
 PIECES = 3 * CAP
 MESH = pl.DeviceIdType.MESH
-STARTS = (0, 224, 336, 384, 608, 720, 768)
+STARTS = (0, 208, 320, 384, 592, 704, 768)
 CHUNKS = 6
 
 FIRST, SECOND = (0, 29), (29, 28)

time: 90.7 us -> 90.3 us (level)
  no operation moved by 1% of the time
where the time goes in v5:
time: 90.3 us; the launch traced here: 90.2 us
  Pallas kernels  88.8 us (98%)
  local copies, waits for them, and re-layouts  1.41 us (2%)
    pallas_call x1, Pallas kernels, body(): pl.pallas_call(main_kernel, out_shape=pltpu.VMEM((768, 768), jnp.float32)...  88.8 us

profile of v5, /device:TPU:1, one launch (start us, length us, event | category | flops | bytes accessed | tf_op | source)
XLA Modules:
  0.0 90.2 jit_solution(16985224350804702864)
XLA Ops:
  0.0 88.8 %ladder.1 = f32[768,768]{1,0:T(8,128)S(1)} custom-call(s32[64,64]{1,0:T(8,128)} %flags_hbm.1, f32[768,768]{1,0:T(8,128)} %amp_hbm.1, f32[768,384]{1,0:T(8,128)} %x_hbm.1), custom_call_target="tpu_custom_call" | custom-call | tf_op jit(solution)/shard_map/ladder/pallas_call | solution.py:396
  88.8 1.4 %copy.5 = f32[768,768]{1,0:T(8,128)} copy(f32[768,768]{1,0:T(8,128)S(1)} %ladder.1) | data formatting | bytes 4718592

commit v6 on v5

--- a/solution.py
+++ b/solution.py
@@ -176,7 +176,7 @@
                     piece = tile[q * PIECE : (q + 1) * PIECE]
                     tiles[3 * (8 * j + i) + q] = jnp.where(free, pltpu.roll(last, 96 - 32 * q, 1), piece)
 
-        @pl.loop(0, CAP)
+        @pl.loop(0, CAP, unroll=True)
         def _(t):
             chosen = jnp.int32(0)
             for j in range(4):

time: 90.3 us -> 90.3 us (level)
  no operation moved by 1% of the time
where the time goes in v6:
time: 90.3 us; the launch traced here: 90.2 us
  Pallas kernels  88.8 us (98%)
  local copies, waits for them, and re-layouts  1.41 us (2%)
    pallas_call x1, Pallas kernels, body(): pl.pallas_call(main_kernel, out_shape=pltpu.VMEM((768, 768), jnp.float32)...  88.8 us

profile of v6, /device:TPU:1, one launch (start us, length us, event | category | flops | bytes accessed | tf_op | source)
XLA Modules:
  0.0 90.2 jit_solution(8642494598032453001)
XLA Ops:
  0.0 88.8 %ladder.1 = f32[768,768]{1,0:T(8,128)S(1)} custom-call(s32[64,64]{1,0:T(8,128)} %flags_hbm.1, f32[768,768]{1,0:T(8,128)} %amp_hbm.1, f32[768,384]{1,0:T(8,128)} %x_hbm.1), custom_call_target="tpu_custom_call" | custom-call | tf_op jit(solution)/shard_map/ladder/pallas_call | solution.py:396
  88.8 1.4 %copy.5 = f32[768,768]{1,0:T(8,128)} copy(f32[768,768]{1,0:T(8,128)S(1)} %ladder.1) | data formatting | bytes 4718592
